TPU v7x, 32 devices: a whole 2x2x4 slice. The times are simulated.
32 devices in a mesh: shard: 2 (over core), rep: 16 (over z, y, x).
Axes of the slice: x: 2, y: 2, z: 4, core: 2. Of those that a mesh axis runs over, the one named last changes fastest.
Arguments:
- tokens: bfloat16 [128, 512, 768], P(('shard', 'rep')), may hold values from -6 to 6
- teacher: bfloat16 [128, 512, 768], P(('shard', 'rep')), may hold values from -6 to 6
- block_ids: int32 [128, 512], P(('shard', 'rep')), may hold values from 0 to 3, never falling along the last dimension, each value on 1 to 256 neighbouring positions
- qkv_weight: bfloat16 [768, 2304], P('shard'), may hold values from -0.21875 to 0.21875
- out_weight: bfloat16 [768, 768], P('shard'), may hold values from -0.875 to 0.875
- up_weight: bfloat16 [768, 3072], P('shard'), may hold values from -0.21875 to 0.21875
- down_weight: bfloat16 [3072, 768], P('shard'), may hold values from -0.109375 to 0.109375
- biases: bfloat16 [768, 4], P('shard'), may hold values from -1.5 to 1.5
- hidden_bias: bfloat16 [3072], P('shard'), may hold values from -1.5 to 1.5
- norm_gain: bfloat16 [768, 2], P('shard'), may hold values from 0.25 to 1.75
- norm_shift: bfloat16 [768, 2], P('shard'), may hold values from -1.5 to 1.5
Outputs:
- layer_out: bfloat16 [128, 512, 768], P(('shard', 'rep'))
- token_grad: float32 [128, 512, 768], P(('shard', 'rep'))
- qkv_grad: float32 [768, 2304], P('shard')
- out_grad: float32 [768, 768], P('shard')
- up_grad: float32 [768, 3072], P('shard')
- down_grad: float32 [3072, 768], P('shard')
- bias_grad: float32 [768, 4], P('shard')
- hidden_grad: float32 [3072], P('shard')
- gain_grad: float32 [768, 2], P('shard')
- shift_grad: float32 [768, 2], P('shard')
Inputs may be any that keep to these rules, and one draw needn't show every extreme that they name: `block_ids`: along each sequence the block ids never fall; each block has 1 to 256 tokens and some block has exactly 256.
All inputs are finite; a program needn't handle non-finite values.
Results may differ from a plain program's by a relative error of at most 0.01.
Values may be sent and summed in bfloat16 or wider, within the bound.
A program may use at most 384 MiB of HBM per device.

v0:
```python
import functools

import jax
import jax.numpy as jnp
from jax import lax
from jax.experimental import pallas as pl
from jax.experimental.pallas import tpu as pltpu
from jax.sharding import PartitionSpec as P

HEAD_DIM = 64
GROUP = 256
EPS = 1e-05
NEG = -1e30
BF = jnp.bfloat16
F32 = jnp.float32
MB = 1 << 20


def params(mb=56, **kw):
    return pltpu.CompilerParams(vmem_limit_bytes=mb * MB, **kw)


def dot(a, b):
    return jnp.dot(a, b, preferred_element_type=F32)


def dot_nt(a, b):
    return lax.dot_general(a, b, (((1,), (1,)), ((), ())), preferred_element_type=F32)


def dot_tn(a, b):
    return lax.dot_general(a, b, (((0,), (0,)), ((), ())), preferred_element_type=F32)


def full(shape):
    return pl.BlockSpec(shape, lambda *_: (0,) * len(shape))


def cost(flops, nbytes, trans=0):
    return pl.CostEstimate(flops=int(flops), bytes_accessed=int(nbytes), transcendentals=int(trans))


def column(row):
    return jnp.broadcast_to(row.astype(F32), (8, row.shape[1])).T[:, 0:1]


def deal(core, acc, mine_ref, theirs_ref, at=0):
    half = acc.shape[0] // 2
    wide = acc.shape[1] // 2
    for ref, who in ((mine_ref, core), (theirs_ref, 1 - core)):
        rows = pl.ds(pl.multiple_of(who * half, half), half)
        ref[at, 0:half, :] = acc[rows, 0:wide].astype(BF)
        ref[at, half : 2 * half, :] = acc[rows, wide : 2 * wide].astype(BF)


def binary_halves(first, second):
    rows = 2 * first.shape[0]
    total = jnp.sum(jnp.abs(first.astype(F32)), axis=0, keepdims=True) + jnp.sum(
        jnp.abs(second.astype(F32)), axis=0, keepdims=True
    )
    scale = (total / rows).astype(BF)
    return (
        jnp.where(first >= 0, scale, -scale).astype(BF),
        jnp.where(second >= 0, scale, -scale).astype(BF),
    )


def binary_rows(core, own_ref, other_ref, out_ref):
    half, cols = own_ref.shape
    own_at = pl.ds(pl.multiple_of(core * half, half), half)
    other_at = pl.ds(pl.multiple_of((1 - core) * half, half), half)
    for j in range(0, cols, GROUP):
        at = slice(j, j + GROUP)
        out_ref[own_at, at], out_ref[other_at, at] = binary_halves(own_ref[:, at], other_ref[:, at])


def binary_up(core, own_ref, other_ref, out_ref):
    half, cols = own_ref.shape
    chunks = cols // (2 * half)
    own_at = pl.ds(pl.multiple_of(core * half, half), half)
    other_at = pl.ds(pl.multiple_of((1 - core) * half, half), half)

    def one(j, _):
        at = pl.ds(pl.multiple_of(j * half, half), half)
        to = pl.ds(pl.multiple_of((j % chunks) * 2 * half + (j // chunks) * half, half), half)
        out_ref[own_at, to], out_ref[other_at, to] = binary_halves(own_ref[:, at], other_ref[:, at])
        return 0

    lax.fori_loop(0, 2 * chunks, one, 0)


def binary_down(core, own_ref, other_ref, out_ref):
    rows, cols = own_ref.shape
    half = cols // 2

    def one(j, _):
        at = pl.ds(pl.multiple_of(j * GROUP, GROUP), GROUP)
        own, other = binary_halves(own_ref[:, at], other_ref[:, at])
        for c in range(rows // half):
            part = slice(c * half, (c + 1) * half)
            out_ref[pl.ds(pl.multiple_of((2 * c + core) * half, half), half), at] = own[part]
            out_ref[pl.ds(pl.multiple_of((2 * c + 1 - core) * half, half), half), at] = other[part]
        return 0

    lax.fori_loop(0, cols // GROUP, one, 0)


def attend_kernel(
    core_ref, tokens_ref, rows_ref, qkv_own, qkv_other, out_own, out_other, small_own, small_other,
    joined_ref, ctx_ref, lse_ref, norm_ref, inv_ref, small_ref, qkv_any, out_any,
    bias_ref, qkv_ref, out_ref, sems,
):
    length, width = tokens_ref.shape[1:]
    keep = (
        pltpu.make_async_copy(qkv_ref, qkv_any, sems.at[0]),
        pltpu.make_async_copy(out_ref, out_any, sems.at[1]),
    )

    @pl.when(pl.program_id(0) == 0)
    def _():
        core, half = core_ref[0], width // 2
        binary_rows(core, qkv_own, qkv_other, qkv_ref)
        binary_rows(core, out_own, out_other, out_ref)
        small_ref[:, pl.ds(pl.multiple_of(core * half, half), half)] = small_own[...].astype(F32)
        small_ref[:, pl.ds(pl.multiple_of((1 - core) * half, half), half)] = small_other[...].astype(F32)
        for copy in keep:
            copy.start()

    x = tokens_ref[0]
    for part, bias_row in ((0, 0), (1, None), (2, 1)):
        joined = dot(x, qkv_ref[:, part * width : (part + 1) * width])
        if bias_row is not None:
            joined = joined + small_ref[bias_row : bias_row + 1, :]
        joined_ref[0, :, part * width : (part + 1) * width] = joined.astype(BF)
    ids = rows_ref[pl.ds(pl.program_id(0), 1), :]
    bias_ref[...] = jnp.where(column(ids) >= ids.astype(F32), 0.0, NEG)
    lane = lax.broadcasted_iota(jnp.int32, (length, 128), 1)
    low = lane < HEAD_DIM
    lse_all = jnp.zeros((length, 128), F32)
    tile = min(TILE_F, length)
    for pair in range(width // 128):
        q2 = joined_ref[0, :, pair * 128 : pair * 128 + 128] * BF(0.125)
        k2 = joined_ref[0, :, width + pair * 128 : width + pair * 128 + 128]
        v2 = joined_ref[0, :, 2 * width + pair * 128 : 2 * width + pair * 128 + 128]
        for t in range(length // tile):
            rows = slice(t * tile, (t + 1) * tile)
            parts = []
            for h in range(2):
                mine = low[rows] if h == 0 else ~low[rows]
                qm = jnp.where(mine, q2[rows], BF(0))
                scores = dot_nt(qm, k2) + bias_ref[rows, :]
                peak = jnp.max(scores, axis=-1, keepdims=True)
                raised = jnp.exp(scores - peak)
                total = jnp.sum(raised, axis=-1, keepdims=True)
                parts.append(dot(raised.astype(BF), v2) / total)
                lse_ref_col = peak + jnp.log(total)
                bias_lane = lane[rows] == 2 * pair + h
                lse_cols = jnp.where(bias_lane, lse_ref_col, 0.0)
                if h == 0:
                    pair_lse = lse_cols
                else:
                    pair_lse = pair_lse + lse_cols
            ctx_ref[0, rows, pair * 128 : pair * 128 + 128] = jnp.where(low[rows], parts[0], parts[1]).astype(BF)
            if t == 0:
                tiles_lse = [pair_lse]
            else:
                tiles_lse.append(pair_lse)
        lse_all = lse_all + jnp.concatenate(tiles_lse, axis=0)
    lse_ref[0] = lse_all.T[0:16, :]
    resid = x.astype(F32) + dot(ctx_ref[0], out_ref[...]) + small_ref[2:3, :]
    center = resid - jnp.mean(resid, axis=-1, keepdims=True)
    inverse = lax.rsqrt(jnp.mean(center * center, axis=-1, keepdims=True) + EPS)
    norm_ref[0] = center * inverse
    inv_ref[0] = inverse

    @pl.when(pl.program_id(0) == pl.num_programs(0) - 1)
    def _():
        for copy in keep:
            copy.wait()


TILE_F = 512


def attend(core, tokens, block_ids, qkv, out, small):
    seqs, length, width = tokens.shape
    per_seq = lambda *shape: pl.BlockSpec((1,) + shape, lambda s, _: (s,) + (0,) * len(shape))
    once = lambda a: pl.BlockSpec(a.shape, lambda s, _: (0,) * a.ndim, pipeline_mode=pl.Buffered(1))
    anywhere = pl.BlockSpec(memory_space=pl.ANY)
    like = jax.ShapeDtypeStruct
    joined_width = qkv[0].shape[1]
    whole = (small[0].shape[0], width)
    return pl.pallas_call(
        attend_kernel,
        grid_spec=pltpu.PrefetchScalarGridSpec(
            num_scalar_prefetch=1,
            grid=(seqs,),
            in_specs=[per_seq(length, width)] + [once(a) for a in (block_ids, *qkv, *out, *small)],
            out_specs=[
                per_seq(length, joined_width),
                per_seq(length, width),
                per_seq(16, length),
                per_seq(length, width),
                per_seq(length, 1),
                full(whole),
                anywhere,
                anywhere,
            ],
            scratch_shapes=[
                pltpu.VMEM((length, length), F32),
                pltpu.VMEM((width, joined_width), BF),
                pltpu.VMEM((width, width), BF),
                pltpu.SemaphoreType.DMA((2,)),
            ],
        ),
        out_shape=[
            like((seqs, length, joined_width), BF),
            like((seqs, length, width), BF),
            like((seqs, 16, length), F32),
            like((seqs, length, width), F32),
            like((seqs, length, 1), F32),
            like(whole, F32),
            like((width, joined_width), BF),
            like((width, width), BF),
        ],
        compiler_params=params(),
        cost_estimate=cost(seqs * length * width * (8 * width + 16 * length), 30 * seqs * length * width),
        name="attend",
    )(core, tokens, block_ids, *qkv, *out, *small)


def gelu_pair(u):
    cdf = 0.5 + 0.5 * lax.erf(u * 0.7071067811865476)
    density = jnp.exp(-0.5 * u * u) * 0.3989422804014327
    return u * cdf, cdf + u * density


def norm_back(upstream, normed, inverse, gain):
    scaled = upstream * gain
    weighted = upstream * normed
    centered = (
        scaled
        - jnp.mean(scaled, axis=-1, keepdims=True)
        - normed * jnp.mean(weighted * gain, axis=-1, keepdims=True)
    )
    return centered * inverse, jnp.sum(weighted, axis=0, keepdims=True), jnp.sum(upstream, axis=0, keepdims=True)


def feed_kernel(
    core_ref, norm_ref, teacher_ref, small_ref, up_own, up_other, dn_own, dn_other,
    final_ref, first_low_ref, hidden_ref, slope_ref, second_ref, mixed_ref, sums_ref, up_any, dn_any,
    up_ref, dn_ref, sems,
):
    width = norm_ref.shape[2]
    keep = (
        pltpu.make_async_copy(up_ref, up_any, sems.at[0]),
        pltpu.make_async_copy(dn_ref, dn_any, sems.at[1]),
    )

    @pl.when(pl.program_id(0) == 0)
    def _():
        binary_up(core_ref[0], up_own, up_other, up_ref)
        binary_down(core_ref[0], dn_own, dn_other, dn_ref)
        for copy in keep:
            copy.start()

    first = norm_ref[0] * small_ref[4:5, :] + small_ref[6:7, :]
    first_low = first.astype(BF)
    first_low_ref[0] = first_low
    acc = first + small_ref[3:4, :]
    for c in range(up_ref.shape[1] // width):
        cols = slice(c * width, (c + 1) * width)
        pre = dot(first_low, up_ref[:, cols]) + small_ref[8 + c : 9 + c, :]
        value, slope = gelu_pair(pre)
        value = value.astype(BF)
        hidden_ref[0, :, cols] = value
        slope_ref[0, :, cols] = slope.astype(BF)
        acc = acc + dot(value, dn_ref[cols, :])
    center = acc - jnp.mean(acc, axis=-1, keepdims=True)
    inverse = lax.rsqrt(jnp.mean(center * center, axis=-1, keepdims=True) + EPS)
    normed = center * inverse
    gain = small_ref[5:6, :]
    final = normed * gain + small_ref[7:8, :]
    final_ref[0] = final.astype(BF)
    upstream = final - teacher_ref[0].astype(F32)
    second, gain_sum, shift_sum = norm_back(upstream, normed, inverse, gain)
    second_ref[0] = second
    mixed_ref[0] = second.astype(BF)

    @pl.when(pl.program_id(0) == 0)
    def _():
        sums_ref[...] = jnp.zeros_like(sums_ref)

    sums_ref[3:4, :] += jnp.sum(second, axis=0, keepdims=True)
    sums_ref[5:6, :] += gain_sum
    sums_ref[7:8, :] += shift_sum

    @pl.when(pl.program_id(0) == pl.num_programs(0) - 1)
    def _():
        for copy in keep:
            copy.wait()


def feed(core, norm, teacher, small, up, dn):
    seqs, length, width = norm.shape
    hidden = up[0].shape[1]
    per_seq = lambda *shape: pl.BlockSpec((1,) + shape, lambda s, _: (s,) + (0,) * len(shape))
    once = lambda a: pl.BlockSpec(a.shape, lambda s, _: (0,) * a.ndim, pipeline_mode=pl.Buffered(1))
    anywhere = pl.BlockSpec(memory_space=pl.ANY)
    like = jax.ShapeDtypeStruct
    row = lambda n, dt: like((seqs, length, n), dt)
    return pl.pallas_call(
        feed_kernel,
        grid_spec=pltpu.PrefetchScalarGridSpec(
            num_scalar_prefetch=1,
            grid=(seqs,),
            in_specs=[per_seq(length, width), per_seq(length, width)] + [once(a) for a in (small, *up, *dn)],
            out_specs=[
                per_seq(length, width),
                per_seq(length, width),
                per_seq(length, hidden),
                per_seq(length, hidden),
                per_seq(length, width),
                per_seq(length, width),
                full((16, width)),
                anywhere,
                anywhere,
            ],
            scratch_shapes=[
                pltpu.VMEM((width, hidden), BF),
                pltpu.VMEM((hidden, width), BF),
                pltpu.SemaphoreType.DMA((2,)),
            ],
        ),
        out_shape=[
            row(width, BF), row(width, BF), row(hidden, BF), row(hidden, BF), row(width, F32), row(width, BF),
            like((16, width), F32), like((width, hidden), BF), like((hidden, width), BF),
        ],
        compiler_params=params(60),
        cost_estimate=cost(4 * seqs * length * width * hidden, 36 * seqs * length * width),
        name="feed",
    )(core, norm, teacher, small, *up, *dn)


def feed_back_kernel(
    core_ref, mixed_ref, first_ref, hidden_ref, slope_ref, dn_ref, sums_in_ref,
    pre_ref, mine_ref, theirs_ref, sums_ref, acc,
):
    chunk = pl.program_id(0)

    @pl.when(chunk == 0)
    def _():
        sums_ref[...] = sums_in_ref[...]

    mixed = mixed_ref[0]
    pre_back = dot_nt(mixed, dn_ref[...]) * slope_ref[0].astype(F32)
    pre_low = pre_back.astype(BF)
    pre_ref[0] = pre_low
    acc[...] = dot_tn(hidden_ref[0], mixed)
    deal(core_ref[0], acc, mine_ref, theirs_ref, 0)
    acc[...] = dot_tn(first_ref[0], pre_low)
    deal(core_ref[0], acc, mine_ref, theirs_ref, 1)
    sums_ref[pl.ds(8 + chunk, 1), :] += jnp.sum(pre_back, axis=0, keepdims=True)


def feed_back(core, mixed, first_low, hidden, slope, dn_bin, sums):
    mixed, first_low, hidden, slope = (a.reshape(1, -1, a.shape[2]) for a in (mixed, first_low, hidden, slope))
    seqs, length, width = mixed.shape
    units = hidden.shape[2]
    chunks = units // width
    return pl.pallas_call(
        feed_back_kernel,
        grid_spec=pltpu.PrefetchScalarGridSpec(
            num_scalar_prefetch=1,
            grid=(chunks,),
            in_specs=[
                pl.BlockSpec((1, length, width), lambda c, _: (0, 0, 0)),
                pl.BlockSpec((1, length, width), lambda c, _: (0, 0, 0)),
                pl.BlockSpec((1, length, width), lambda c, _: (0, 0, c)),
                pl.BlockSpec((1, length, width), lambda c, _: (0, 0, c)),
                pl.BlockSpec((width, width), lambda c, _: (c, 0)),
                full(sums.shape),
            ],
            out_specs=[
                pl.BlockSpec((1, length, width), lambda c, _: (0, 0, c)),
                pl.BlockSpec((2, width, width // 2), lambda c, _: (c, 0, 0)),
                pl.BlockSpec((2, width, width // 2), lambda c, _: (c, 0, 0)),
                full(sums.shape),
            ],
            scratch_shapes=[pltpu.VMEM((width, width), F32)],
        ),
        out_shape=[
            jax.ShapeDtypeStruct((seqs, length, units), BF),
            jax.ShapeDtypeStruct((2 * chunks, width, width // 2), BF),
            jax.ShapeDtypeStruct((2 * chunks, width, width // 2), BF),
            jax.ShapeDtypeStruct(sums.shape, F32),
        ],
        compiler_params=params(),
        cost_estimate=cost(6 * seqs * length * width * units, 20 * seqs * length * units),
        name="feed_back",
    )(core, mixed, first_low, hidden, slope, dn_bin, sums)


def norm_step(second, pre_low, norm, inv, ctx, up_ref, out_ref, small_ref, sums_ref, pause):
    width = second.shape[1]
    back = second + dot_nt(pre_low, up_ref[...])
    pause(1)
    resid, gain_sum, shift_sum = norm_back(back, norm, inv, small_ref[4:5, :])
    sums_ref[2:3, :] += jnp.sum(resid, axis=0, keepdims=True)
    sums_ref[4:5, :] += gain_sum
    sums_ref[6:7, :] += shift_sum
    low = resid.astype(BF)
    cback = dot_nt(low, out_ref[...]).astype(BF)
    prod = cback.astype(F32) * ctx.astype(F32)
    high = prod.astype(BF)
    rest = (prod - high.astype(F32)).astype(BF)
    heads = lax.broadcasted_iota(jnp.int32, (16, width), 0)
    lanes = lax.broadcasted_iota(jnp.int32, (16, width), 1)
    pick = jnp.where((lanes >= heads * HEAD_DIM) & (lanes < heads * HEAD_DIM + HEAD_DIM), 1.0, 0.0).astype(BF)
    return low, cback, dot_nt(pick, high) + dot_nt(pick, rest), dot_tn(ctx, low)


MESH = pl.DeviceIdType.MESH

SMALL = 5

LOTS = (
    (0, 0, 384, "xyz"),
    (1, 0, 384, "yxz"),
    (2, 0, 384, "yxz"),
    (3, 0, 384, "yxz"),
    (4, 0, 384, "yxz"),
    (5, 0, 384, "xyz"),
    (6, 0, 384, "zxy"),
    (7, 0, 384, "yxz"),
    (8, 0, 384, "xyz"),
    (9, 0, 384, "xyz"),
    (10, 0, 384, "xyz"),
    (11, 0, 128, "zxy"),
    (11, 128, 128, "yxz"),
    (11, 256, 128, "yxz"),
)
EVENTS = (
    (),
    ((0, 0), (1, 0), (2, 0), (3, 0),),
    ((4, 0), (5, 0),),
    ((6, 0), (7, 0),),
    ((0, 1), (1, 1),),
    (),
    (),
    ((5, 1),),
    ((2, 1),),
    ((1, 2),),
    (),
    ((2, 2), (3, 1), (6, 1),),
    ((1, 3),),
    (),
    ((2, 3), (3, 2), (4, 1),),
    ((1, 4), (6, 2),),
    (),
    ((2, 4), (4, 2), (7, 1),),
    ((1, 5), (3, 3), (0, 2), (8, 0),),
    (),
    ((2, 5), (4, 3), (6, 3), (5, 2),),
    ((3, 4), (7, 2),),
    ((0, 3),),
    ((1, 6),),
    ((4, 4), (8, 1),),
    ((3, 5), (5, 3),),
    ((2, 6), (6, 4), (9, 0), (4, 5), (7, 3),),
    ((8, 2),),
    ((6, 5), (0, 4),),
    ((5, 4),),
    ((3, 6),),
    ((7, 4), (9, 1),),
    ((8, 3),),
    ((4, 6),),
    ((0, 5), (7, 5), (10, 0),),
    (),
    ((5, 5),),
    ((9, 2),),
    ((0, 6), (6, 6),),
    ((8, 4),),
    ((7, 6), (9, 3), (10, 1), (11, 0), (12, 0), (13, 0), (8, 5), (9, 4), (10, 2), (5, 6), (12, 1), (11, 1), (13, 1), (10, 3), (9, 5), (8, 6), (12, 2), (11, 2), (13, 2), (11, 3), (10, 4), (12, 3), (11, 4), (13, 3), (12, 4), (9, 6), (13, 4), (10, 5), (11, 5), (12, 5), (13, 5), (12, 6), (11, 6), (13, 6), (10, 6),),
)


class Exchange:
    def __init__(self, lots, copied, result_ref, held, from_core, inbox, kept, came, sems):
        (
            local_sem, core_send, core_recv, out_send, out_recv, back_send, back_recv, small_send, small_recv, done_sem
        ) = sems
        self.copied = copied
        core, rep = lax.axis_index("shard"), lax.axis_index("rep")
        place = {"x": rep % 2, "y": (rep // 2) % 2, "z": rep // 4, "p": rep % 4}
        ways = {"x": 2, "y": 2, "z": 4, "p": 4}
        sibling = {"shard": 1 - core}
        rows = held.shape[1]
        step_rows = rows // 16

        def peers(axis):
            if axis == "p":
                return [{"rep": rep - place["p"] + (place["p"] + d) % 4} for d in (1, 2, 3)]
            if axis == "z":
                return [{"rep": rep % 4 + 4 * ((place["z"] + d) % 4)} for d in (1, 2, 3)]
            stride = {"x": 1, "y": 2}[axis]
            return [{"rep": rep + stride - 2 * stride * place[axis]}]

        def meet():
            barrier = pltpu.get_barrier_semaphore()
            everyone = [sibling] + peers("p") + peers("z")
            for peer in everyone:
                pl.semaphore_signal(barrier, inc=1, device_id=peer, device_id_type=MESH)
            pl.semaphore_wait(barrier, len(everyone))

        def send(src, dst, send_sem, recv_sem, peer):
            return pltpu.make_async_remote_copy(
                src_ref=src, dst_ref=dst, send_sem=send_sem, recv_sem=recv_sem, device_id=peer, device_id_type=MESH
            )

        def block(at, size):
            return pl.ds(at if isinstance(at, int) else pl.multiple_of(at, step_rows), size)

        def columns(lot):
            return pl.ds(lots[lot][1], lots[lot][2])

        def chain(lot):
            base, size, inside, sem, out = 0, rows, 0, 0, []
            for axis in lots[lot][3]:
                part = size // ways[axis]
                mine = base + place[axis] * part
                out.append((axis, base, part, mine, inside, sem))
                base, size, inside, sem = mine, part, inside + size - part, sem + ways[axis] - 1
            return out

        def core_copy(lot, theirs=None):
            u, cols = lots[lot][0], columns(lot)
            here = from_core.at[u, :, cols]
            return send(here if theirs is None else theirs.at[:, cols], here, core_send.at[lot], core_recv.at[lot], sibling)

        def out_copies(lot, s):
            u, cols = lots[lot][0], columns(lot)
            axis, base, part, _, inside, sem = chain(lot)[s]
            copies = []
            for n, peer in enumerate(peers(axis)):
                away = base + ((place[axis] + n + 1) % ways[axis]) * part
                copy = send(
                    held.at[u, block(away, part), cols], inbox.at[u, block(inside + n * part, part), cols],
                    out_send.at[lot, sem + n], out_recv.at[lot, sem + n], peer,
                )
                copies.append((away, copy))
            return copies

        def back_copies(lot, s):
            u, cols = lots[lot][0], columns(lot)
            axis, _, part, mine, _, sem = chain(lot)[s]
            own = from_core.at[u, block(mine, part), cols]
            return [
                send(own, own, back_send.at[lot, sem + n], back_recv.at[lot, sem + n], peer)
                for n, peer in enumerate(peers(axis))
            ]

        def done_copy(lot):
            u, cols = lots[lot][0], columns(lot)
            return pltpu.make_async_copy(from_core.at[u, :, cols], result_ref.at[u, :, cols], done_sem.at[lot])

        def add(lot, at, size, terms, target):
            u, cols = lots[lot][0], columns(lot)
            some = min(size, rows // 4)

            def one(n, _):
                total = held[u, block(at + n * some, some), cols].astype(F32)
                for ref, shift in terms:
                    total = total + ref[u, block(at + shift + n * some, some), cols].astype(F32)
                target[u, block(at + n * some, some), cols] = total.astype(BF)
                return 0

            if size == some:
                one(0, 0)
            else:
                lax.fori_loop(0, size // some, one, 0)

        def fire(lot, k):
            links = chain(lot)
            last = len(links)
            if k == 0:
                core_copy(lot).wait_recv()
                if lot < self.copied:
                    pltpu.make_async_copy(from_core.at[lot], held.at[lot], local_sem.at[lot]).wait()
                terms = [(from_core, 0)]
            elif k <= last:
                for _, copy in out_copies(lot, k - 1):
                    copy.wait_recv()
                axis, _, part, mine, inside, _ = links[k - 1]
                terms = [(inbox, inside + n * part - mine) for n in range(ways[axis] - 1)]
            if k < last:
                _, _, part, mine, _, _ = links[k]
                for away, copy in out_copies(lot, k):
                    add(lot, away, part, terms, held)
                    copy.start()
                add(lot, mine, part, terms, held)
                return
            if k == last:
                _, _, part, mine, _, _ = links[k - 1]
                add(lot, mine, part, terms, from_core)
            else:
                for copy in back_copies(lot, 2 * last - k):
                    copy.wait_recv()
            if k < 2 * last:
                for copy in back_copies(lot, 2 * last - 1 - k):
                    copy.start()
            else:
                done_copy(lot).start()

        def begin(u, theirs, mine=None):
            for lot in range(len(lots)):
                if lots[lot][0] == u:
                    core_copy(lot, theirs).start()
            if mine is not None:
                pltpu.make_async_copy(mine, held.at[u], local_sem.at[u]).start()

        small_peers = [
            sibling, peers("x")[0], peers("y")[0],
            {"rep": rep + 4 - 8 * (place["z"] % 2)}, {"rep": rep + 8 - 16 * (place["z"] // 2)},
        ]

        def copy_small(k):
            return send(kept.at[k], came.at[k], small_send.at[k], small_recv.at[k], small_peers[k])

        def small_next(k):
            copy_small(k).wait_recv()
            kept[k + 1] = kept[k] + came[k]
            if k + 1 < SMALL:
                copy_small(k + 1).start()

        def settle():
            for k in range(SMALL):
                copy_small(k).wait_send()
            for lot in range(len(lots)):
                core_copy(lot).wait_send()
                for s in range(len(lots[lot][3])):
                    for _, copy in out_copies(lot, s):
                        copy.wait_send()
                    for copy in back_copies(lot, s):
                        copy.wait_send()
                done_copy(lot).wait()

        self.meet, self.begin, self.fire, self.settle = meet, begin, fire, settle
        self.small_start, self.small_next = (lambda: copy_small(0).start()), small_next

    @staticmethod
    def buffers(lots, units, rows, cols, small):
        dma = pltpu.SemaphoreType.DMA
        count = len(lots)
        return [
            pltpu.VMEM((units, rows, cols), BF),
            pltpu.VMEM((units, rows, cols), BF),
            pltpu.VMEM((units, rows - rows // 16, cols), BF),
            pltpu.VMEM((SMALL + 1,) + small, F32),
            pltpu.VMEM((SMALL,) + small, F32),
            dma((units,)), dma((count,)), dma((count,)),
        ] + [dma((count, 6))] * 4 + [dma((SMALL,))] * 2 + [dma((count,))]


HALVES = 2
TILE_B = 256


def late_back_kernel(linked, seqs, groups, *refs):
    (
        second_ref, pre_ref, norm_ref, inv_ref, ctx_ref, up_ref, out_ref, small_ref,
        tokens_ref, rows_ref, q_ref, k_ref, v_ref, lse_ref, sums_in_ref,
    ), refs = refs[:15], refs[15:]
    step = pl.program_id(0)
    last = pl.num_programs(0) - 1
    first = seqs * HALVES
    if linked:
        feed_mine, feed_theirs, resid_ref, jlow_ref, result_ref, total_ref = refs[:6]
        cback_ref, rowdot_ref, acc, bias_ref, theirs = refs[6:11]
        buffers, sems = refs[11:16], refs[16:]
        early = feed_mine.shape[0]
        exchange = Exchange(LOTS, early, result_ref, *buffers, sems)
        held, kept = buffers[0], buffers[3]
        core = lax.axis_index("shard")
        sums_ref = kept.at[0]
    else:
        resid_ref, jlow_ref, mine_ref, theirs_ref, sums_ref, cback_ref, rowdot_ref, acc, bias_ref = refs

    def pause(start, count, each, n):
        for i in range(count if linked else 0):
            events = EVENTS[start[1] + each * i + n]
            if events:

                @pl.when(step == start[0] + i)
                def _():
                    for lot, k in events:
                        exchange.fire(lot, k)

    pause_norm = functools.partial(pause, (0, 0), first, 2)
    pause_attend = functools.partial(pause, (first, 2 * first), seqs * groups, 2)

    def hand_over(n):
        if linked:
            deal(core, acc, held.at[pl.ds(early + n, 1)], theirs.at[pl.ds(n, 1)])
            for m in range(1 + groups):

                @pl.when(n == m)
                def _():
                    exchange.begin(early + m, theirs.at[m])

        else:
            deal(0, acc, mine_ref.at[pl.ds(n, 1)], theirs_ref.at[pl.ds(n, 1)])

    @pl.when(step == 0)
    def _():
        if linked:
            exchange.meet()
            for u in range(early):
                exchange.begin(u, feed_theirs.at[u], feed_mine.at[u])
        sums_ref[...] = sums_in_ref[...]

    @pl.when(step < first)
    def _():
        pause_norm(0)
        resid, cback, rowdot, part = norm_step(
            second_ref[0], pre_ref[0], norm_ref[0], inv_ref[0], ctx_ref[0], up_ref, out_ref, small_ref, sums_ref,
            pause_norm,
        )
        resid_ref[0] = resid
        size = resid.shape[0]
        s, some = step // HALVES, pl.ds(pl.multiple_of(step % HALVES * size, size), size)
        for n in range(groups):
            cback_ref[s, n, some, :] = cback[:, n * GROUP : (n + 1) * GROUP]
        rowdot_ref[s, :, some] = rowdot

        @pl.when(step == 0)
        def _():
            acc[...] = part

        @pl.when(step > 0)
        def _():
            acc[...] += part

        @pl.when(step == first - 1)
        def _():
            hand_over(step - (first - 1))

    @pl.when(step >= first)
    def _():
        g, s = (step - first) // seqs, (step - first) % seqs
        attend_step(
            g, s, tokens_ref, rows_ref, q_ref, k_ref, v_ref, cback_ref, lse_ref, rowdot_ref,
            jlow_ref, sums_ref, bias_ref, acc, pause_attend,
        )

        @pl.when(s == seqs - 1)
        def _():
            hand_over(1 + g)

    if linked:

        @pl.when(step == last)
        def _():
            exchange.small_start()
            rest = EVENTS[-1]
            share = -(-len(rest) // (SMALL + 1))
            for k in range(SMALL + 1):
                for lot, stage in rest[k * share : (k + 1) * share]:
                    exchange.fire(lot, stage)
                if k < SMALL:
                    exchange.small_next(k)
            total_ref[...] = kept[SMALL]
            exchange.settle()


def attend_step(
    g, s, tokens_ref, rows_ref, q_ref, k_ref, v_ref, cback_ref, lse_ref, rowdot_ref,
    jlow_ref, sums_ref, bias_ref, acc, pause,
):
    length = tokens_ref.shape[1]
    tile = min(TILE_B, length)
    ids = rows_ref[pl.ds(s, 1), :]
    bias_ref[...] = jnp.where(ids.astype(F32) >= column(ids), 0.0, NEG)
    lane = lax.broadcasted_iota(jnp.int32, (length, 128), 1)
    low = lane < HEAD_DIM

    for pair in range(GROUP // 128):
        pause(pair)
        at = slice(pair * 128, pair * 128 + 128)
        q2 = q_ref[0, :, at] * BF(0.125)
        k2 = k_ref[0, :, at]
        v2 = v_ref[0, :, at]
        do2 = cback_ref[s, g, :, at]
        dq = None
        for t in range(length // tile):
            rows = slice(t * tile, (t + 1) * tile)
            dks, dvs = [], []
            for h in range(2):
                mine = low[rows] if h == 0 else ~low[rows]
                km = jnp.where(mine, k2[rows], BF(0))
                vm = jnp.where(mine, v2[rows], BF(0))
                head = g * (GROUP // HEAD_DIM) + pair * 2 + h
                lse = lse_ref[0, pl.ds(head, 1), :]
                rowdot = rowdot_ref[s, pl.ds(head, 1), :]
                probs = jnp.exp(dot_nt(km, q2) + bias_ref[rows, :] - lse)
                dprobs = dot_nt(vm, do2)
                dscore = (probs * (dprobs - rowdot)).astype(BF)
                dvs.append(dot(probs.astype(BF), do2))
                dks.append(dot(dscore, q2))
                part = dot_tn(dscore, km * BF(0.125))
                dq = part if dq is None else dq + part
            dk = jnp.where(low[rows], dks[0], dks[1])
            dv = jnp.where(low[rows], dvs[0], dvs[1])
            jlow_ref[0, rows, GROUP + pair * 128 : GROUP + pair * 128 + 128] = dk.astype(BF)
            jlow_ref[0, rows, 2 * GROUP + pair * 128 : 2 * GROUP + pair * 128 + 128] = dv.astype(BF)
            vsum = jnp.sum(dv, axis=0, keepdims=True)
            vtotal = vsum if t == 0 else vtotal + vsum
        jlow_ref[0, :, at] = dq.astype(BF)
        lanes = pl.ds(pl.multiple_of(g * GROUP + pair * 128, 128), 128)
        sums_ref[0:1, lanes] += jnp.sum(dq, axis=0, keepdims=True)
        sums_ref[1:2, lanes] += vtotal

    part = dot_tn(tokens_ref[0], jlow_ref[0])

    @pl.when(s == 0)
    def _():
        acc[...] = part

    @pl.when(s > 0)
    def _():
        acc[...] += part


def late_back(second, pre_low, norm, inv, ctx, up_bin, out_bin, small, tokens, block_ids, joined, lse, sums, feed_grads=None):
    seqs, length, width = tokens.shape
    groups = width // GROUP
    linked = feed_grads is not None
    first = seqs * HALVES
    phase = lambda i: (i + 64 - first) // 64
    seq_one = lambda i: i + phase(i) * (first - 1 - i)
    seq_two = lambda i: phase(i) * ((i - first + seqs * first) % seqs)
    group_two = lambda i: phase(i) * ((i - first) // seqs)
    some = length // HALVES
    second, pre_low, norm, inv, ctx = (a.reshape(first, some, a.shape[2]) for a in (second, pre_low, norm, inv, ctx))
    one = lambda *shape: pl.BlockSpec((1,) + shape, lambda i: (seq_one(i),) + (0,) * len(shape))
    two = lambda *shape: pl.BlockSpec((1,) + shape, lambda i: (seq_two(i),) + (0,) * len(shape))
    part = lambda k: pl.BlockSpec((1, length, GROUP), lambda i: (seq_two(i), 0, k * groups + group_two(i)))
    held = lambda a: pl.BlockSpec(a.shape, lambda i: (0,) * a.ndim, pipeline_mode=pl.Buffered(1))
    anywhere = pl.BlockSpec(memory_space=pl.ANY)
    unit = (width, width // 2)
    like = jax.ShapeDtypeStruct
    in_specs = [
        one(some, width), one(some, pre_low.shape[2]), one(some, width), one(some, 1), one(some, width),
        held(up_bin), held(out_bin), held(small),
        two(length, width), held(block_ids), part(0), part(1), part(2), two(16, length), held(sums),
    ]
    operands = [
        second, pre_low, norm, inv, ctx, up_bin, out_bin, small,
        tokens, block_ids, joined, joined, joined, lse, sums,
    ]
    out_specs = [one(some, width), pl.BlockSpec((1, length, 3 * GROUP), lambda i: (seq_two(i), 0, group_two(i)))]
    out_shape = [like((first, some, width), BF), like((seqs, length, 3 * width), BF)]
    scratch = [
        pltpu.VMEM((seqs, groups, length, GROUP), BF), pltpu.VMEM((seqs, 16, length), F32),
        pltpu.VMEM((width, width), F32), pltpu.VMEM((length, length), F32),
    ]
    if linked:
        units = feed_grads[0].shape[0] + 1 + groups
        in_specs += [anywhere] * 2
        operands += feed_grads
        out_specs += [anywhere, full(sums.shape)]
        out_shape += [like((units,) + unit, BF), like(sums.shape, F32)]
        scratch += [pltpu.VMEM((1 + groups,) + unit, BF)] + Exchange.buffers(LOTS, units, *unit, sums.shape)
        extra = dict(collective_id=0, has_side_effects=True)
    else:
        out_specs += [full((1 + groups,) + unit)] * 2 + [full(sums.shape)]
        out_shape += [like((1 + groups,) + unit, BF)] * 2 + [like(sums.shape, F32)]
        extra = {}
    return pl.pallas_call(
        functools.partial(late_back_kernel, linked, seqs, groups),
        grid=(seqs * (HALVES + groups),),
        in_specs=in_specs,
        out_specs=out_specs,
        out_shape=out_shape,
        scratch_shapes=scratch,
        compiler_params=params(58, **extra),
        cost_estimate=cost(seqs * length * width * (20 * width + 40 * length), 70 * seqs * length * width),
        name="late_back",
    )(*operands)


def token_total(resid_ref, jlow_ref, qkv_ref):
    width = resid_ref.shape[2]
    groups = width // GROUP
    total = resid_ref[0].astype(F32)
    for g in range(groups):
        for k in range(3):
            at = (3 * g + k) * GROUP
            col = k * width + g * GROUP
            total = total + dot_nt(jlow_ref[0, :, at : at + GROUP], qkv_ref[:, col : col + GROUP])
    return total


def token_kernel(resid_ref, jlow_ref, qkv_ref, grad_ref):
    grad_ref[0] = token_total(resid_ref, jlow_ref, qkv_ref)


def finish_kernel(
    core_ref, resid_ref, jlow_ref, qkv_bin_ref, feed_ref, out_unit_ref, qkv_unit_ref, sums_ref,
    grad_ref, qkv_ref, out_ref, up_ref, dn_ref, small_ref, up_stage, qkv_stage, up_sem, qkv_sem,
):
    step, last = pl.program_id(0), pl.num_programs(0) - 1
    _, rows, half = feed_ref.shape
    groups = qkv_sem.shape[0]
    parts = (slice(0, half), slice(half, rows))

    def up_copy(c, p):
        at = pl.ds(pl.multiple_of((p * (last + 1) + c) * half, half), half)
        return pltpu.make_async_copy(up_stage.at[c, p], up_ref.at[:, at], up_sem.at[c, p])

    def qkv_copy(g, k):
        at = pl.ds(pl.multiple_of(k * rows + g * GROUP, GROUP), GROUP)
        return pltpu.make_async_copy(qkv_stage.at[g, k], qkv_ref.at[:, at], qkv_sem.at[g, k])

    for p in range(2):
        up_stage[step, p] = feed_ref[1, parts[p], :].astype(F32)
        up_copy(step, p).start()
        dn_ref[:, parts[p]] = feed_ref[0, parts[p], :].astype(F32)

    @pl.when(step == 0)
    def _():
        for p in range(2):
            out_ref[:, parts[p]] = out_unit_ref[0, parts[p], :].astype(F32)
        mine = pl.ds(pl.multiple_of(core_ref[0] * half, half), half)
        small_ref[...] = sums_ref[:, mine]

    @pl.when(step > 0)
    def _():
        for j in range(3 * GROUP // 128):
            col = j * 128
            qkv_stage[step - 1, col // GROUP, :, col % GROUP : col % GROUP + 128] = qkv_unit_ref[
                0, parts[col // half], col % half : col % half + 128
            ].astype(F32)
        for k in range(3):
            qkv_copy(step - 1, k).start()

    grad_ref[0] = token_total(resid_ref, jlow_ref, qkv_bin_ref)

    @pl.when(step == last)
    def _():
        for c in range(up_sem.shape[0]):
            for p in range(2):
                up_copy(c, p).wait()
        for g in range(groups):
            for k in range(3):
                qkv_copy(g, k).wait()


def finish(core, resid, jlow, qkv_bin, units, sums):
    seqs, length, width = resid.shape
    count, rows, half = units.shape
    groups = rows // GROUP
    chunks = (count - 1 - groups) // 2
    assert chunks == seqs and groups == seqs - 1
    per_seq = lambda *shape: pl.BlockSpec((1,) + shape, lambda s, _: (s,) + (0,) * len(shape))
    late = lambda s: s - (s + 63) // 64
    like = lambda *shape: jax.ShapeDtypeStruct(shape, F32)
    anywhere = pl.BlockSpec(memory_space=pl.ANY)
    return pl.pallas_call(
        finish_kernel,
        grid_spec=pltpu.PrefetchScalarGridSpec(
            num_scalar_prefetch=1,
            grid=(chunks,),
            in_specs=[
                per_seq(length, width),
                per_seq(length, 3 * width),
                full(qkv_bin.shape),
                pl.BlockSpec((2, rows, half), lambda s, _: (s, 0, 0)),
                pl.BlockSpec((1, rows, half), lambda s, _: (2 * chunks, 0, 0)),
                pl.BlockSpec((1, rows, half), lambda s, _: (2 * chunks + 1 + late(s), 0, 0)),
                full(sums.shape),
            ],
            out_specs=[
                per_seq(length, width),
                anywhere,
                full((half, rows)),
                anywhere,
                pl.BlockSpec((half, rows), lambda s, _: (s, 0)),
                full((sums.shape[0], half)),
            ],
            scratch_shapes=[
                pltpu.VMEM((chunks, 2, half, half), F32),
                pltpu.VMEM((groups, 3, half, GROUP), F32),
                pltpu.SemaphoreType.DMA((chunks, 2)),
                pltpu.SemaphoreType.DMA((groups, 3)),
            ],
        ),
        out_shape=[
            like(seqs, length, width), like(half, 3 * rows), like(half, rows), like(half, 2 * chunks * half),
            like(chunks * half, rows), like(sums.shape[0], half),
        ],
        compiler_params=params(),
        cost_estimate=cost(6 * seqs * length * width * width, 16 * seqs * length * width),
        name="finish",
    )(core, resid, jlow, qkv_bin, units, units, units, sums)


def token_back(resid, jlow, qkv_bin):
    seqs, length, width = resid.shape
    per_seq = lambda *shape: pl.BlockSpec((1,) + shape, lambda s: (s,) + (0,) * len(shape))
    return pl.pallas_call(
        token_kernel,
        grid=(seqs,),
        in_specs=[per_seq(length, width), per_seq(length, 3 * width), full(qkv_bin.shape)],
        out_specs=per_seq(length, width),
        out_shape=jax.ShapeDtypeStruct((seqs, length, width), F32),
        compiler_params=params(),
        cost_estimate=cost(6 * seqs * length * width * width, 16 * seqs * length * width),
        name="token_back",
    )(resid, jlow, qkv_bin)


def swap(value):
    return lax.ppermute(value, "shard", [(0, 1), (1, 0)])


def small_rows(biases, gain, shift, hidden_bias):
    rows = biases.shape[0]
    return jnp.concatenate([biases.T, gain.T, shift.T, hidden_bias.reshape(-1, rows)], axis=0)


def reduce_plain(feed_grads, out_grads, qkv_grads, sums):
    def whole(mine, theirs):
        count, rows, half = mine.shape
        cut = lambda a: a.reshape(count, 2, half, half).transpose(0, 2, 1, 3).reshape(count, half, rows)
        return jnp.concatenate([cut(mine), cut(theirs)], axis=1)

    feed_all, out_all, qkv_all = whole(*feed_grads), whole(*out_grads), whole(*qkv_grads)
    chunks, groups, width = feed_all.shape[0] // 2, qkv_all.shape[0], feed_all.shape[2]
    half, units = width // 2, chunks * width
    grads = (
        qkv_all.reshape(groups, width, 3, GROUP).transpose(1, 2, 0, 3).reshape(width, 3 * width),
        out_all[0],
        feed_all[1::2].reshape(chunks, width, 2, half).transpose(1, 2, 0, 3).reshape(width, units),
        feed_all[0::2].reshape(chunks, 2, half, width).transpose(1, 0, 2, 3).reshape(units, width),
        sums[0:4].T.astype(BF),
        sums[8:].reshape(chunks, 2, half).transpose(1, 0, 2).reshape(-1).astype(BF),
        sums[4:6].T.astype(BF),
        sums[6:8].T.astype(BF),
    )
    owned = lax.psum_scatter(grads, "shard", scatter_dimension=0, tiled=True)
    return jax.tree.map(lambda part: part.astype(F32), lax.psum(owned, "rep"))


def body(tokens, teacher, block_ids, *weights):
    qkv, out, up, down, biases, hidden_bias, gain, shift = weights
    paired = lax.axis_size("shard") == 2 and lax.axis_size("rep") == 16
    if paired:
        core = lax.axis_index("shard").reshape(1)
        small = small_rows(biases, gain, shift, hidden_bias)
        small, qkv, out = ((a, swap(a)) for a in (small, qkv, out))
        up, down, _, _ = lax.optimization_barrier((up, down, qkv[1], small[1]))
        up, down = ((a, swap(a)) for a in (up, down))
    else:
        core = jnp.zeros((1,), jnp.int32)
        gathered = [lax.all_gather(w, "shard", axis=0, tiled=True) for w in weights]
        qkv, out, up, down, *rest = (jnp.split(w, 2, axis=0) for w in gathered)
        small = [small_rows(rest[0][i], rest[2][i], rest[3][i], rest[1][i]) for i in range(2)]
    joined, ctx, lse, norm, inv, small, qkv_bin, out_bin = attend(core, tokens, block_ids, qkv, out, small)
    final, first_low, hidden, slope, second, mixed, sums, up_bin, dn_bin = feed(core, norm, teacher, small, up, down)
    pre_low, *feed_grads, sums = feed_back(core, mixed, first_low, hidden, slope, dn_bin, sums)
    pre_low = pre_low.reshape(hidden.shape)
    operands = (second, pre_low, norm, inv, ctx, up_bin, out_bin, small, tokens, block_ids, joined, lse, sums)
    if not paired:
        resid, jlow, *grads, sums = late_back(*operands)
        token_grad = token_back(resid.reshape(tokens.shape), jlow, qkv_bin)
        out_grads, qkv_grads = ([a[cut] for a in grads] for cut in (slice(0, 1), slice(1, None)))
        return (final, token_grad) + tuple(reduce_plain(feed_grads, out_grads, qkv_grads, sums[:12]))
    resid, jlow, units, sums = late_back(*operands, feed_grads)
    resid = resid.reshape(tokens.shape)
    token_grad, qkv_grad, out_grad, up_grad, dn_grad, small = finish(core, resid, jlow, qkv_bin, units, sums)
    hidden_rows = hidden_bias.shape[0] // small.shape[1]
    return (
        final, token_grad, qkv_grad, out_grad, up_grad, dn_grad,
        small[0:4].T, small[8 : 8 + hidden_rows].reshape(-1), small[4:6].T, small[6:8].T,
    )


def solution(mesh):
    placed = (
        P(("shard", "rep"), None, None),
        P(("shard", "rep"), None, None),
        P(("shard", "rep"), None),
        P("shard", None),
        P("shard", None),
        P("shard", None),
        P("shard", None),
        P("shard", None),
        P("shard"),
        P("shard", None),
        P("shard", None),
    )
    return jax.shard_map(
        body,
        mesh=mesh,
        in_specs=placed,
        out_specs=placed[:2] + placed[3:],
        check_vma=False,
    )
```

profile of v0, /device:TPU:0, one launch (start us, length us, event | category | flops | bytes accessed | tf_op | source)
XLA Modules:
  0.0 304.8 jit_solution(4710847168981883027)
XLA Ops:
  0.6 0.5 collective-permute-start
  1.2 0.1 collective-permute-start.1
  1.2 0.7 reshape.57
  1.9 0.7 pad_maximum_fusion.small_own
  2.7 0.0 copy-start
  2.7 0.5 collective-permute-start.2
  3.2 1.3 collective-permute-done.2.small_other
  4.5 0.0 copy-start.3
  4.5 1.2 collective-permute-done.qkv_other
  5.7 0.4 collective-permute-start.3
  6.1 0.1 collective-permute-start.4
  6.2 0.0 collective-permute-done.1.out_other
  6.2 0.0 copy-start.2
  6.2 0.0 copy-done
  6.2 0.0 copy-done.3
  6.2 0.8 copy-done.2
  7.0 36.9 %attend.1 = (bf16[4,512,2304]{2,1,0:T(8,128)(2,1)}, bf16[4,512,768]{2,1,0:T(8,128)(2,1)}, f32[4,16,512]{2,1,0:T(8,128)}, f32[4,512,768]{2,1,0:T(8,128)}, f32[4,5...) custom-call(s32[1]{0:T(128)} %bitcast.core_ref, ...), custom_call_target="tpu_custom_call" | custom-call | flops 22548578304 | bytes 47185920 | tf_op jit(solution)/shard_map/attend/pallas_call | solution.py:193
  44.0 0.0 collective-permute-done.3.up_other
  44.0 0.0 copy-start.1
  44.0 0.0 collective-permute-done.4.dn_other
  44.0 1.3 copy-done.1
  45.3 42.0 %feed.1 = (bf16[4,512,768]{2,1,0:T(8,128)(2,1)}, bf16[4,512,768]{2,1,0:T(8,128)(2,1)}, bf16[4,512,3072]{2,1,0:T(8,128)(2,1)}, bf16[4,512,3072]{2,1,0:T(8,128)(2,...) custom-call(s32[1]{0:T(128)} %bitcast.core_ref, ...), custom_call_target="tpu_custom_call" | custom-call | flops 19327352832 | bytes 56623104 | tf_op jit(solution)/shard_map/feed/pallas_call | solution.py:312
  87.3 38.6 %feed_back.1 = (bf16[1,2048,3072]{2,1,0:T(8,128)(2,1)}, bf16[8,768,384]{2,1,0:T(8,128)(2,1)}, bf16[8,768,384]{2,1,0:T(8,128)(2,1)}, f32[16,768]{1,0:T(8,128)}) custom-call(s32[1]{0:T(128)} %bitcast.core_ref, bf16[1,2048,768]{2,1,0:T(8,128)(2,1)} %bitcast.31, bf16[1,2048,768]{2,1,0:T(8,128)(2,1)} %bitcast.30, bf16[1,2048,3072]{2,1,0:T(8,128)(2,1)} %bitcast.25, ...), custom_call_target="tpu_custom_call" | custom-call | flops 28991029248 | bytes 125829120 | tf_op jit(solution)/shard_map/feed_back/pallas_call | solution.py:371
  125.9 156.8 %late_back.1 = (bf16[8,256,768]{2,1,0:T(8,128)(2,1)}, bf16[4,512,2304]{2,1,0:T(8,128)(2,1)}, bf16[12,768,384]{2,1,0:T(8,128)(2,1)}, f32[16,768]{1,0:T(8,128)}) custom-call(f32[8,256,768]{2,1,0:T(8,128)} %bitcast.28, bf16[8,256,3072]{2,1,0:T(8,128)(2,1)} %bitcast.24, f32[8,256,768]{2,1,0:T(8,128)} %bitcast.27, f32[8,256,1]{2,1,0:T(8,128)} %bitcast.32, ...), custom_call_target="tpu_custom_call" | custom-call | flops 56371445760 | bytes 110100480 | tf_op jit(solution)/shard_map/late_back/pallas_call | solution.py:879
  282.7 18.6 %finish.1 = (f32[4,512,768]{2,1,0:T(8,128)}, f32[384,2304]{1,0:T(8,128)}, f32[384,768]{1,0:T(8,128)}, f32[384,3072]{1,0:T(8,128)}, f32[1536,768]{1,0:T(8,128)}, /*index=5*/f32[16,384]{1,0:T(8,128)}) custom-call(s32[1]{0:T(128)} %bitcast.core_ref, bf16[4,512,768]{2,1,0:T(8,128)(2,1)} %bitcast.20, bf16[4,512,2304]{2,1,0:T(8,128)(2,1)} %get-tuple-element.66.jlow_ref, ...), custom_call_target="tpu_custom_call" | custom-call | flops 7247757312 | bytes 25165824 | tf_op jit(solution)/shard_map/finish/pallas_call | solution.py:969
  301.3 1.4 slice_bitcast_fusion.1
  302.6 1.3 fusion
  303.9 0.6 reshape.67
Async XLA Ops:
  0.6 5.0 %collective-permute-start = (bf16[384,2304]{1,0:T(8,128)(2,1)}, bf16[384,2304]{1,0:T(8,128)(2,1)}, u32[]{:S(2)}, u32[]{:S(2)}) collective-permute-start(bf16[384,2304]{1,0:T(8,128)(2,1)} %qkv_own.1), channel_id=1, source_target_pairs={{0,16},{16,0},{1,17},{17,1},{2,18},{18,2},{3,19},{19,3},{4,20},{20... | collective-permute-start | bytes 5308424 | tf_op jit(solution)/shard_map/ppermute | solution.py:1024
  1.2 5.0 %collective-permute-start.1 = (bf16[384,768]{1,0:T(8,128)(2,1)}, bf16[384,768]{1,0:T(8,128)(2,1)S(1)}, u32[]{:S(2)}, u32[]{:S(2)}) collective-permute-start(bf16[384,768]{1,0:T(8,128)(2,1)} %out_own.1), channel_id=1, source_target_pairs={{0,16},{16,0},{1,17},{17,1},{2,18},{18,2},{3,19},{19,3},{4,20},{20... | collective-permute-start | bytes 1769480 | tf_op jit(solution)/shard_map/ppermute | solution.py:1024
  2.7 3.5 %copy-start = (bf16[12,384]{1,0:T(8,128)(2,1)}, bf16[12,384]{1,0:T(8,128)(2,1)S(1)}, u32[]{:S(2)}) copy-start(bf16[12,384]{1,0:T(8,128)(2,1)S(1)} %pad_maximum_fusion.small_own) | copy-start | bytes 27652
  2.7 1.8 collective-permute-start.2
  4.5 1.7 copy-start.3
  5.7 38.3 %collective-permute-start.3 = (bf16[384,3072]{1,0:T(8,128)(2,1)}, bf16[384,3072]{1,0:T(8,128)(2,1)S(1)}, u32[]{:S(2)}, u32[]{:S(2)}) collective-permute-start(bf16[384,3072]{1,0:T(8,128)(2,1)} %up_own), channel_id=1, source_target_pairs={{0,16},{16,0},{1,17},{17,1},{2,18},{18,2},{3,19},{19,3},{4,20},{20... | collective-permute-start | bytes 7077896 | tf_op jit(solution)/shard_map/ppermute | solution.py:1024
  6.1 37.9 %collective-permute-start.4 = (bf16[1536,768]{1,0:T(8,128)(2,1)}, bf16[1536,768]{1,0:T(8,128)(2,1)}, u32[]{:S(2)}, u32[]{:S(2)}) collective-permute-start(bf16[1536,768]{1,0:T(8,128)(2,1)} %dn_own), channel_id=1, source_target_pairs={{0,16},{16,0},{1,17},{17,1},{2,18},{18,2},{3,19},{19,3},{4,20},{20... | collective-permute-start | bytes 7077896 | tf_op jit(solution)/shard_map/ppermute | solution.py:1024
  6.2 0.8 copy-start.2
  44.0 1.4 copy-start.1
where the time goes:
time: 308 us; the launch traced here: 305 us
  Pallas kernels  293 us (95%)
  local copies, waits for them, and re-layouts  6.16 us (2%)
    pallas_call x1, Pallas kernels, late_back(): pl.pallas_call(functools.partial(late_back_kernel, linked, seqs, groups),...  157 us
    pallas_call x1, Pallas kernels, feed(): pl.pallas_call(feed_kernel, grid_spec=pltpu.PrefetchScalarGridSpec(num_sc...  42 us
    pallas_call x1, Pallas kernels, feed_back(): pl.pallas_call(feed_back_kernel, grid_spec=pltpu.PrefetchScalarGridSpec(n...  38.6 us
    pallas_call x1, Pallas kernels, attend(): pl.pallas_call(attend_kernel, grid_spec=pltpu.PrefetchScalarGridSpec(num_...  36.9 us
    pallas_call x1, Pallas kernels, finish(): pl.pallas_call(finish_kernel, grid_spec=pltpu.PrefetchScalarGridSpec(num_...  18.6 us
  transfers between devices with their start and end apart: 5, of which 2 were waited for; matrix products, arithmetic and copies ran while one was open for 0% of the time, Pallas kernels for 12%

commit v1 on v0

--- a/solution.py
+++ b/solution.py
@@ -907,9 +907,10 @@
 
 def finish_kernel(
     core_ref, resid_ref, jlow_ref, qkv_bin_ref, feed_ref, out_unit_ref, qkv_unit_ref, sums_ref,
-    grad_ref, qkv_ref, out_ref, up_ref, dn_ref, small_ref, up_stage, qkv_stage, up_sem, qkv_sem,
+    grad_ref, qkv_ref, out_ref, up_ref, dn_ref, bias_ref, hidden_ref, gain_ref, shift_ref,
+    up_stage, qkv_stage, up_sem, qkv_sem,
 ):
-    step, last = pl.program_id(0), pl.num_programs(0) - 1
+    step, last = pl.program_id(0), up_sem.shape[0] - 1
     _, rows, half = feed_ref.shape
     groups = qkv_sem.shape[0]
     parts = (slice(0, half), slice(half, rows))
@@ -932,7 +933,14 @@
         for p in range(2):
             out_ref[:, parts[p]] = out_unit_ref[0, parts[p], :].astype(F32)
         mine = pl.ds(pl.multiple_of(core_ref[0] * half, half), half)
-        small_ref[...] = sums_ref[:, mine]
+        total = sums_ref[:, mine]
+        bias_ref[...] = total[0:4]
+        gain_ref[...] = total[4:6]
+        shift_ref[...] = total[6:8]
+        for c in range(last + 1):
+            for j in range(half // 128):
+                at = c * (half // 128) + j
+                hidden_ref[at : at + 1, :] = total[8 + c : 9 + c, j * 128 : (j + 1) * 128]
 
     @pl.when(step > 0)
     def _():
@@ -986,7 +994,10 @@
                 full((half, rows)),
                 anywhere,
                 pl.BlockSpec((half, rows), lambda s, _: (s, 0)),
-                full((sums.shape[0], half)),
+                full((4, half)),
+                full((chunks * half // 128, 128)),
+                full((2, half)),
+                full((2, half)),
             ],
             scratch_shapes=[
                 pltpu.VMEM((chunks, 2, half, half), F32),
@@ -997,7 +1008,7 @@
         ),
         out_shape=[
             like(seqs, length, width), like(half, 3 * rows), like(half, rows), like(half, 2 * chunks * half),
-            like(chunks * half, rows), like(sums.shape[0], half),
+            like(chunks * half, rows), like(4, half), like(chunks * half // 128, 128), like(2, half), like(2, half),
         ],
         compiler_params=params(),
         cost_estimate=cost(6 * seqs * length * width * width, 16 * seqs * length * width),
@@ -1078,12 +1089,8 @@
         return (final, token_grad) + tuple(reduce_plain(feed_grads, out_grads, qkv_grads, sums[:12]))
     resid, jlow, units, sums = late_back(*operands, feed_grads)
     resid = resid.reshape(tokens.shape)
-    token_grad, qkv_grad, out_grad, up_grad, dn_grad, small = finish(core, resid, jlow, qkv_bin, units, sums)
-    hidden_rows = hidden_bias.shape[0] // small.shape[1]
-    return (
-        final, token_grad, qkv_grad, out_grad, up_grad, dn_grad,
-        small[0:4].T, small[8 : 8 + hidden_rows].reshape(-1), small[4:6].T, small[6:8].T,
-    )
+    token_grad, *grads, bias, hidden, gains, shifts = finish(core, resid, jlow, qkv_bin, units, sums)
+    return (final, token_grad, *grads, bias.T, hidden.reshape(-1), gains.T, shifts.T)
 
 
 def solution(mesh):

time: 308 us -> 304 us (0.987)
  local copies, waits for them, and re-layouts: 6.16 us -> 2.87 us
where the time goes in v1:
time: 304 us; the launch traced here: 302 us
  Pallas kernels  293 us (96%)
    pallas_call x1, Pallas kernels, late_back(): pl.pallas_call(functools.partial(late_back_kernel, linked, seqs, groups),...  157 us
    pallas_call x1, Pallas kernels, feed(): pl.pallas_call(feed_kernel, grid_spec=pltpu.PrefetchScalarGridSpec(num_sc...  41.9 us
    pallas_call x1, Pallas kernels, feed_back(): pl.pallas_call(feed_back_kernel, grid_spec=pltpu.PrefetchScalarGridSpec(n...  38.6 us
    pallas_call x1, Pallas kernels, attend(): pl.pallas_call(attend_kernel, grid_spec=pltpu.PrefetchScalarGridSpec(num_...  36.9 us
    pallas_call x1, Pallas kernels, finish(): pl.pallas_call(finish_kernel, grid_spec=pltpu.PrefetchScalarGridSpec(num_...  18.6 us
  transfers between devices with their start and end apart: 5, of which 2 were waited for; matrix products, arithmetic and copies ran while one was open for 0% of the time, Pallas kernels for 12%

profile of v1, /device:TPU:0, one launch (start us, length us, event | category | flops | bytes accessed | tf_op | source)
XLA Modules:
  0.0 301.5 jit_solution(1844228066882263295)
XLA Ops:
  0.6 0.5 collective-permute-start
  1.2 0.1 collective-permute-start.1
  1.2 0.7 reshape.57
  1.9 0.7 pad_maximum_fusion.small_own
  2.7 0.0 copy-start
  2.7 0.5 collective-permute-start.2
  3.2 1.3 collective-permute-done.2.small_other
  4.5 0.0 copy-start.3
  4.5 1.2 collective-permute-done.qkv_other
  5.7 0.4 collective-permute-start.3
  6.1 0.1 collective-permute-start.4
  6.2 0.0 collective-permute-done.1.out_other
  6.2 0.0 copy-start.2
  6.2 0.0 copy-done
  6.2 0.0 copy-done.3
  6.2 0.8 copy-done.2
  7.0 36.9 %attend.1 = (bf16[4,512,2304]{2,1,0:T(8,128)(2,1)}, bf16[4,512,768]{2,1,0:T(8,128)(2,1)}, f32[4,16,512]{2,1,0:T(8,128)}, f32[4,512,768]{2,1,0:T(8,128)}, f32[4,5...) custom-call(s32[1]{0:T(128)} %bitcast.core_ref, ...), custom_call_target="tpu_custom_call" | custom-call | flops 22548578304 | bytes 47185920 | tf_op jit(solution)/shard_map/attend/pallas_call | solution.py:193
  44.0 0.0 collective-permute-done.3.up_other
  44.0 0.0 copy-start.1
  44.0 0.0 collective-permute-done.4.dn_other
  44.0 1.4 copy-done.1
  45.4 41.9 %feed.1 = (bf16[4,512,768]{2,1,0:T(8,128)(2,1)}, bf16[4,512,768]{2,1,0:T(8,128)(2,1)}, bf16[4,512,3072]{2,1,0:T(8,128)(2,1)}, bf16[4,512,3072]{2,1,0:T(8,128)(2,...) custom-call(s32[1]{0:T(128)} %bitcast.core_ref, ...), custom_call_target="tpu_custom_call" | custom-call | flops 19327352832 | bytes 56623104 | tf_op jit(solution)/shard_map/feed/pallas_call | solution.py:312
  87.3 38.6 %feed_back.1 = (bf16[1,2048,3072]{2,1,0:T(8,128)(2,1)}, bf16[8,768,384]{2,1,0:T(8,128)(2,1)}, bf16[8,768,384]{2,1,0:T(8,128)(2,1)}, f32[16,768]{1,0:T(8,128)}) custom-call(s32[1]{0:T(128)} %bitcast.core_ref, bf16[1,2048,768]{2,1,0:T(8,128)(2,1)} %bitcast.33, bf16[1,2048,768]{2,1,0:T(8,128)(2,1)} %bitcast.32, bf16[1,2048,3072]{2,1,0:T(8,128)(2,1)} %bitcast.27, ...), custom_call_target="tpu_custom_call" | custom-call | flops 28991029248 | bytes 125829120 | tf_op jit(solution)/shard_map/feed_back/pallas_call | solution.py:371
  125.9 156.8 %late_back.1 = (bf16[8,256,768]{2,1,0:T(8,128)(2,1)}, bf16[4,512,2304]{2,1,0:T(8,128)(2,1)}, bf16[12,768,384]{2,1,0:T(8,128)(2,1)}, f32[16,768]{1,0:T(8,128)}) custom-call(f32[8,256,768]{2,1,0:T(8,128)} %bitcast.30, bf16[8,256,3072]{2,1,0:T(8,128)(2,1)} %bitcast.26, f32[8,256,768]{2,1,0:T(8,128)} %bitcast.29, f32[8,256,1]{2,1,0:T(8,128)} %bitcast.34, ...), custom_call_target="tpu_custom_call" | custom-call | flops 56371445760 | bytes 110100480 | tf_op jit(solution)/shard_map/late_back/pallas_call | solution.py:879
  282.7 18.6 %finish.1 = (f32[4,512,768]{2,1,0:T(8,128)}, f32[384,2304]{1,0:T(8,128)}, f32[384,768]{1,0:T(8,128)}, f32[384,3072]{1,0:T(8,128)}, f32[1536,768]{1,0:T(8,128)}, ...) custom-call(s32[1]{0:T(128)} %bitcast.core_ref, bf16[4,512,768]{2,1,0:T(8,128)(2,1)} %bitcast.18, ...), custom_call_target="tpu_custom_call" | custom-call | flops 7247757312 | bytes 25165824 | tf_op jit(solution)/shard_map/finish/pallas_call | solution.py:977
Async XLA Ops:
  0.6 5.0 %collective-permute-start = (bf16[384,2304]{1,0:T(8,128)(2,1)}, bf16[384,2304]{1,0:T(8,128)(2,1)}, u32[]{:S(2)}, u32[]{:S(2)}) collective-permute-start(bf16[384,2304]{1,0:T(8,128)(2,1)} %qkv_own.1), channel_id=1, source_target_pairs={{0,16},{16,0},{1,17},{17,1},{2,18},{18,2},{3,19},{19,3},{4,20},{20... | collective-permute-start | bytes 5308424 | tf_op jit(solution)/shard_map/ppermute | solution.py:1035
  1.2 5.0 %collective-permute-start.1 = (bf16[384,768]{1,0:T(8,128)(2,1)}, bf16[384,768]{1,0:T(8,128)(2,1)S(1)}, u32[]{:S(2)}, u32[]{:S(2)}) collective-permute-start(bf16[384,768]{1,0:T(8,128)(2,1)} %out_own.1), channel_id=1, source_target_pairs={{0,16},{16,0},{1,17},{17,1},{2,18},{18,2},{3,19},{19,3},{4,20},{20... | collective-permute-start | bytes 1769480 | tf_op jit(solution)/shard_map/ppermute | solution.py:1035
  2.7 3.5 %copy-start = (bf16[12,384]{1,0:T(8,128)(2,1)}, bf16[12,384]{1,0:T(8,128)(2,1)S(1)}, u32[]{:S(2)}) copy-start(bf16[12,384]{1,0:T(8,128)(2,1)S(1)} %pad_maximum_fusion.small_own) | copy-start | bytes 27652
  2.7 1.8 collective-permute-start.2
  4.5 1.7 copy-start.3
  5.7 38.3 %collective-permute-start.3 = (bf16[384,3072]{1,0:T(8,128)(2,1)}, bf16[384,3072]{1,0:T(8,128)(2,1)S(1)}, u32[]{:S(2)}, u32[]{:S(2)}) collective-permute-start(bf16[384,3072]{1,0:T(8,128)(2,1)} %up_own), channel_id=1, source_target_pairs={{0,16},{16,0},{1,17},{17,1},{2,18},{18,2},{3,19},{19,3},{4,20},{20... | collective-permute-start | bytes 7077896 | tf_op jit(solution)/shard_map/ppermute | solution.py:1035
  6.1 37.9 %collective-permute-start.4 = (bf16[1536,768]{1,0:T(8,128)(2,1)}, bf16[1536,768]{1,0:T(8,128)(2,1)}, u32[]{:S(2)}, u32[]{:S(2)}) collective-permute-start(bf16[1536,768]{1,0:T(8,128)(2,1)} %dn_own), channel_id=1, source_target_pairs={{0,16},{16,0},{1,17},{17,1},{2,18},{18,2},{3,19},{19,3},{4,20},{20... | collective-permute-start | bytes 7077896 | tf_op jit(solution)/shard_map/ppermute | solution.py:1035
  6.2 0.8 copy-start.2
  44.0 1.4 copy-start.1
